TPU v7x, 512 devices: a whole 4x4x16 slice. The times are simulated.
512 devices in a mesh: dp: 64 (over y, z), mp: 8 (over x, core).
Axes of the slice: x: 4, y: 4, z: 16, core: 2. Of those that a mesh axis runs over, the one named last changes fastest.
Arguments:
- x_in: bfloat16 [25600, 2048], P('dp'), may hold values from -6 to 6
- cotangent: bfloat16 [25600, 7168], P('dp', 'mp'), may hold values from -6 to 6
- w_gate: bfloat16 [2048, 7168], P('dp', 'mp'), may hold values from -0.125 to 0.125
- w_up: bfloat16 [2048, 7168], P('dp', 'mp'), may hold values from -0.125 to 0.125
- send_counts: int32 [64, 64], P('dp'), may hold values from 0 to 4, as said below
- recv_counts: int32 [64, 64], P('dp'), may hold values from 0 to 4, as said below
Outputs:
- grad_x: bfloat16 [25600, 2048], P('dp', 'mp')
- grad_gate: float32 [2048, 7168], P('dp', 'mp')
Inputs may be any that keep to these rules, and one draw needn't show every extreme that they name: `send_counts`: each entry is 0 to 4. A quarter of the indices only send and the rest only receive; one sending index sends 4 rows to every receiver, so its live rows reach 400. recv_counts is the transpose of send_counts.
All inputs are finite; a program needn't handle non-finite values.
Results may differ from a plain program's by a relative error of at most 0.014.
Values may be sent and summed in bfloat16 or wider, within the bound.
A program may use at most 64 MiB of HBM per device.

v0:
```python
import jax
import jax.numpy as jnp
from jax import lax
from jax.sharding import PartitionSpec as P

BAL = 208


def contract_last(left, right):
    return lax.dot_general(
        left, right, (((1,), (1,)), ((), ())), preferred_element_type=jnp.float32
    )


def swiglu_back(x_rows, cot_rows, gate_full, up_full, live_mask):
    gate_val = jnp.dot(x_rows, gate_full, preferred_element_type=jnp.float32)
    up_val = jnp.dot(x_rows, up_full, preferred_element_type=jnp.float32)
    sig = jax.nn.sigmoid(gate_val)
    cot_val = cot_rows.astype(jnp.float32)
    d_gate = jnp.where(
        live_mask[:, None], cot_val * up_val * sig * (1.0 + gate_val * (1.0 - sig)), 0.0
    ).astype(jnp.bfloat16)
    d_up = jnp.where(live_mask[:, None], cot_val * gate_val * sig, 0.0).astype(jnp.bfloat16)
    partial_value = contract_last(d_gate, gate_full) + contract_last(d_up, up_full)
    return (partial_value, d_gate)


def group_sum(partial_value):
    return lax.psum_scatter(
        partial_value.astype(jnp.bfloat16), "mp", scatter_dimension=1, tiled=True
    )


def on_device(x_in, cotangent, w_gate, w_up, send_counts, recv_counts):
    rows_cap = x_in.shape[0]
    width = x_in.shape[1]
    dev_count = lax.axis_size("dp")
    gate_full, up_full = (
        lax.all_gather(w_gate, "dp", axis=0, tiled=True),
        lax.all_gather(w_up, "dp", axis=0, tiled=True),
    )
    sent = send_counts[0]
    got = recv_counts[0]
    live_rows = BAL + jnp.sum(sent) - jnp.sum(got)
    live_mask = jnp.arange(rows_cap) < live_rows
    partial_value, d_gate = swiglu_back(x_in, cotangent, gate_full, up_full, live_mask)
    grad_x = group_sum(partial_value)
    block_rows = width // dev_count
    whole = lax.dot_general(
        x_in, d_gate, (((0,), (0,)), ((), ())), preferred_element_type=jnp.float32
    )
    grad_gate = lax.psum_scatter(
        whole.astype(jnp.bfloat16), "dp", scatter_dimension=0, tiled=True
    ).astype(jnp.float32)
    return (grad_x, grad_gate)


def solution(mesh):
    return jax.shard_map(
        on_device,
        mesh=mesh,
        in_specs=(
            P("dp", None),
            P("dp", "mp"),
            P("dp", "mp"),
            P("dp", "mp"),
            P("dp", None),
            P("dp", None),
        ),
        out_specs=(P("dp", "mp"), P("dp", "mp")),
        check_vma=False,
    )
```

profile of v0, /device:TPU:8, one launch (start us, length us, event | category | flops | bytes accessed | tf_op | source)
XLA Modules:
  0.0 1060.5 jit_solution(8219626550588682840)
XLA Ops:
  7.2 0.0 copy-start
  7.2 0.0 all-gather.5.cloned.1.call-start
  7.2 0.7 all-gather.5.cloned.1.call-update
  7.9 0.0 all-gather.3.cloned.1.call-start
  8.0 0.7 all-gather.3.cloned.1.call-update
  8.7 0.0 reduce-scatter.7.cloned.1.call-start
  8.7 1.3 reduce_sum.19
  10.0 1.3 reduce_sum.18
  12.6 0.0 copy-start.2
  12.6 147.1 %all-gather.5.cloned.1.call-done = bf16[2048,896]{1,0:T(8,128)(2,1)} async-done(((bf16[32,896]{1,0:T(8,128)(2,1)}), bf16[2048,896]{1,0:T(8,128)(2,1)}) %all-gather.5.cloned.1.call-update) | async-done | bytes 3670032 | tf_op jit(solution)/shard_map/all_gather | solution.py:39
  159.7 5.0 fusion.11
  164.7 137.7 %all-gather.3.cloned.1.call-done = bf16[2048,896]{1,0:T(8,128)(2,1)} async-done(((bf16[32,896]{1,0:T(8,128)(2,1)}), bf16[2048,896]{1,0:T(8,128)(2,1)}) %all-gather.3.cloned.1.call-update) | async-done | bytes 3670032 | tf_op jit(solution)/shard_map/all_gather | solution.py:40
  302.4 4.6 select_convert_fusion
  307.0 4.0 convert_bitcast_fusion
  311.0 6.1 copy.10
  317.1 0.0 reduce-scatter.7.cloned.1.call-update
  317.2 0.0 reduce-scatter.5.cloned.1.call-start
  317.2 4.1 fusion.12
  321.3 3.1 add_convert_fusion
  324.5 0.0 reduce-scatter.5.cloned.1.call-update
  324.5 687.3 %reduce-scatter.7.cloned.1.call-done = bf16[32,896]{1,0:T(8,128)(2,1)} async-done(((bf16[2048,896]{1,0:T(8,128)(2,1)}), bf16[32,896]{1,0:T(8,128)(2,1)}) %reduce-scatter.7.cloned.1.call-update) | async-done | bytes 57360
  1011.7 1.0 copy.11
  1012.7 0.8 copy.9
  1013.5 40.4 %reduce-scatter.5.cloned.1.call-done = bf16[400,256]{1,0:T(8,128)(2,1)} async-done(((bf16[400,2048]{1,0:T(8,128)(2,1)}), bf16[400,256]{1,0:T(8,128)(2,1)}) %reduce-scatter.5.cloned.1.call-update) | async-done | bytes 204816 | tf_op jit(solution)/shard_map/reduce_scatter | solution.py:29
  (7 shorter events, 0.0 us)
Async XLA Ops:
  7.2 152.6 %copy-start = (bf16[400,2048]{1,0:T(8,128)(2,1)S(1)}, bf16[400,2048]{1,0:T(8,128)(2,1)}, u32[]{:S(2)}) copy-start(bf16[400,2048]{1,0:T(8,128)(2,1)} %param.6) | copy-start | bytes 4915204
  7.2 152.5 %all-gather.5.cloned.1.call-start = ((), (), s32[]{:S(2)}) async-start(), calls=%async_computation.3 | async-start | bytes 3727360 | tf_op jit(solution)/shard_map/all_gather | solution.py:39
  7.9 294.5 %all-gather.3.cloned.1.call-start = ((), (), s32[]{:S(2)}) async-start(), calls=%async_computation.2 | async-start | bytes 3727360 | tf_op jit(solution)/shard_map/all_gather | solution.py:40
  8.7 1003.1 %reduce-scatter.7.cloned.1.call-start = ((), (), s32[]{:S(2)}) async-start(), calls=%async_computation.5 | async-start | bytes 3727360
  12.6 289.8 %copy-start.2 = (bf16[400,896]{1,0:T(8,128)(2,1)S(1)}, bf16[400,896]{1,0:T(8,128)(2,1)}, u32[]{:S(2)}) copy-start(bf16[400,896]{1,0:T(8,128)(2,1)} %param.7) | copy-start | bytes 2150404
  317.2 736.8 %reduce-scatter.5.cloned.1.call-start = ((), (), s32[]{:S(2)}) async-start(), calls=%async_computation.4 | async-start | bytes 1843200 | tf_op jit(solution)/shard_map/reduce_scatter | solution.py:29
  317.2 4.1 copy-start.1
  317.2 4.1 copy-start.3
Sparse Core Ops, SparseCore 0:
  11.0 148.7 all-gather.4
  162.7 139.7 all-gather.2
  317.3 694.4 reduce-scatter.6
  1015.3 38.6 reduce-scatter.4
where the time goes:
time: 1060 us
  waiting for transfers between devices  1010 us (95%)
  matrix products  20.8 us (2%)
  between operations  15.1 us (1%)
    unnamed x5, waiting for transfers between devices  689 us
    all_gather x1, waiting for transfers between devices, on_device(): lax.all_gather(w_gate, 'dp', axis=0, tiled=True)  147 us
    all_gather x1, waiting for transfers between devices, on_device(): lax.all_gather(w_up, 'dp', axis=0, tiled=True)  138 us
    reduce_scatter x1, waiting for transfers between devices, group_sum(): lax.psum_scatter(partial_value.astype(jnp.bfloat16), 'mp', scatter_dimens...  40.4 us
  transfers between devices with their start and end apart: 4, of which 4 were waited for; matrix products, arithmetic and copies ran while one was open for 2% of the time, Pallas kernels for 0%

commit v1 on v0

--- a/solution.py
+++ b/solution.py
@@ -4,6 +4,11 @@
 from jax.sharding import PartitionSpec as P
 
 BAL = 208
+
+
+def gather_from_all(shard, axis, dim):
+    copies = jnp.concatenate([shard] * lax.axis_size(axis), axis=dim)
+    return lax.all_to_all(copies, axis, dim, dim, tiled=True)
 
 
 def contract_last(left, right):
@@ -37,7 +42,7 @@
     dev_count = lax.axis_size("dp")
     gate_full, up_full = (
         lax.all_gather(w_gate, "dp", axis=0, tiled=True),
-        lax.all_gather(w_up, "dp", axis=0, tiled=True),
+        gather_from_all(w_up, "dp", 0),
     )
     sent = send_counts[0]
     got = recv_counts[0]

time: 1060 us -> 1020 us (0.962)
  waiting for transfers between devices: 1010 us -> 925 us
  local copies, waits for them, and re-layouts: 7.91 us -> 36.9 us
  starting transfers between devices: 0.16 us -> 19.2 us
    all_gather x1 -> x0, waiting for transfers between devices: 138 us -> none  [on_device(): lax.all_gather(w_up, 'dp', axis=0, tiled=True)]
    all_gather x1, waiting for transfers between devices: 147 us -> 198 us  [on_device(): lax.all_gather(w_gate, 'dp', axis=0, tiled=True)]
    unnamed x11 -> x80, local copies, waits for them, and re-layouts: 7.91 us -> 36.9 us
    all_to_all x0 -> x1, starting transfers between devices: none -> 19 us  [gather_from_all(): return lax.all_to_all(copies, axis, dim, dim, tiled=True)]
    unnamed x5 -> x4, waiting for transfers between devices: 689 us -> 687 us
  transfers between devices with their start and end apart: 4 -> 4, of which waited for: 4 -> 3; matrix products, arithmetic and copies ran while one was open for 2% -> 2% of each run, Pallas kernels for 0% -> 0%
where the time goes in v1:
time: 1020 us
  waiting for transfers between devices  925 us (91%)
  local copies, waits for them, and re-layouts  36.9 us (4%)
  matrix products  22.8 us (2%)
  starting transfers between devices  19.2 us (2%)
  between operations  15.3 us (2%)
    unnamed x4, waiting for transfers between devices  687 us
    all_gather x1, waiting for transfers between devices, on_device(): lax.all_gather(w_gate, 'dp', axis=0, tiled=True)  198 us
    reduce_scatter x1, waiting for transfers between devices, group_sum(): lax.psum_scatter(partial_value.astype(jnp.bfloat16), 'mp', scatter_dimens...  40.5 us
    unnamed x80, local copies, waits for them, and re-layouts  36.9 us
  transfers between devices with their start and end apart: 4, of which 3 were waited for; matrix products, arithmetic and copies ran while one was open for 2% of the time, Pallas kernels for 0%

profile of v1, /device:TPU:8, one launch (start us, length us, event | category | flops | bytes accessed | tf_op | source)
XLA Modules:
  0.0 1020.2 jit_solution(2516748521423423073)
XLA Ops:
  7.2 1.0 constant_dynamic-update-slice_fusion.63
  8.2 0.8 constant_dynamic-update-slice_fusion.62
  9.0 0.8 constant_dynamic-update-slice_fusion.61
  9.8 0.8 constant_dynamic-update-slice_fusion.60
  10.6 0.8 constant_dynamic-update-slice_fusion.59
  11.5 0.8 constant_dynamic-update-slice_fusion.58
  12.3 0.8 constant_dynamic-update-slice_fusion.57
  13.1 0.8 constant_dynamic-update-slice_fusion.56
  14.0 0.8 constant_dynamic-update-slice_fusion.55
  14.8 0.8 constant_dynamic-update-slice_fusion.54
  15.6 0.8 constant_dynamic-update-slice_fusion.53
  16.5 0.8 constant_dynamic-update-slice_fusion.52
  34.4 1.9 copy-done.2
  36.4 19.0 %all-to-all-start = ((bf16[64,32,896]{2,1,0:T(8,128)(2,1)}), bf16[64,32,896]{2,1,0:T(8,128)(2,1)}, u32[]{:S(2)}, u32[]{:S(2)}) async-start(bf16[64,32,896]{2,1,0:T(8,128)(2,1)} %bitcast.24), calls=%async_computation | async-start | bytes 7340032 | tf_op jit(solution)/shard_map/all_to_all | solution.py:11
  58.8 197.7 %all-gather.2.cloned.1.call-done = bf16[2048,896]{1,0:T(8,128)(2,1)} async-done(((bf16[32,896]{1,0:T(8,128)(2,1)}), bf16[2048,896]{1,0:T(8,128)(2,1)}) %all-gather.2.cloned.1.call-update) | async-done | bytes 3670032 | tf_op jit(solution)/shard_map/all_gather | solution.py:44
  256.5 5.0 fusion.11
  261.5 4.6 select_convert_fusion
  266.1 4.0 convert_bitcast_fusion
  270.1 6.1 copy.10
  276.3 4.0 fusion.12
  280.4 5.1 add_convert_fusion
  285.6 685.9 %reduce-scatter.7.cloned.1.call-done = bf16[32,896]{1,0:T(8,128)(2,1)} async-done(((bf16[2048,896]{1,0:T(8,128)(2,1)}), bf16[32,896]{1,0:T(8,128)(2,1)}) %reduce-scatter.7.cloned.1.call-update) | async-done | bytes 57360
  971.5 1.0 copy.11
  973.2 40.5 %reduce-scatter.5.cloned.1.call-done = bf16[400,256]{1,0:T(8,128)(2,1)} async-done(((bf16[400,2048]{1,0:T(8,128)(2,1)}), bf16[400,256]{1,0:T(8,128)(2,1)}) %reduce-scatter.5.cloned.1.call-update) | async-done | bytes 204816 | tf_op jit(solution)/shard_map/reduce_scatter | solution.py:34
  (76 shorter events, 19.9 us)
Async XLA Ops:
  7.2 249.3 %copy-start = (bf16[400,2048]{1,0:T(8,128)(2,1)S(1)}, bf16[400,2048]{1,0:T(8,128)(2,1)}, u32[]{:S(2)}) copy-start(bf16[400,2048]{1,0:T(8,128)(2,1)} %param.6) | copy-start | bytes 4915204
  7.2 26.7 %copy-start.1 = (bf16[32,896]{1,0:T(8,128)(2,1)S(1)}, bf16[32,896]{1,0:T(8,128)(2,1)}, u32[]{:S(2)}) copy-start(bf16[32,896]{1,0:T(8,128)(2,1)} %param.9) | copy-start | bytes 172036
  34.4 1.9 copy-start.2
  36.4 19.8 %copy-start.4 = (s32[1,64]{1,0:T(1,128)S(1)}, s32[1,64]{1,0:T(1,128)}, u32[]{:S(2)}) copy-start(s32[1,64]{1,0:T(1,128)} %param.11) | copy-start | bytes 772
  36.4 20.5 %copy-start.5 = (s32[1,64]{1,0:T(1,128)S(1)}, s32[1,64]{1,0:T(1,128)}, u32[]{:S(2)}) copy-start(s32[1,64]{1,0:T(1,128)} %param.10) | copy-start | bytes 772
  36.4 225.2 %all-to-all-start = ((bf16[64,32,896]{2,1,0:T(8,128)(2,1)}), bf16[64,32,896]{2,1,0:T(8,128)(2,1)}, u32[]{:S(2)}, u32[]{:S(2)}) async-start(bf16[64,32,896]{2,1,0:T(8,128)(2,1)} %bitcast.24), calls=%async_computation | async-start | bytes 7340032 | tf_op jit(solution)/shard_map/all_to_all | solution.py:11
  55.4 201.1 %all-gather.2.cloned.1.call-start = ((), (), s32[]{:S(2)}) async-start(), calls=%async_computation.3 | async-start | bytes 3727360 | tf_op jit(solution)/shard_map/all_gather | solution.py:44
  56.1 915.3 %reduce-scatter.7.cloned.1.call-start = ((), (), s32[]{:S(2)}) async-start(), calls=%async_computation.5 | async-start | bytes 3727360
  58.8 202.8 %copy-start.3 = (bf16[400,896]{1,0:T(8,128)(2,1)S(1)}, bf16[400,896]{1,0:T(8,128)(2,1)}, u32[]{:S(2)}) copy-start(bf16[400,896]{1,0:T(8,128)(2,1)} %param.7) | copy-start | bytes 2150404
  276.3 737.4 %reduce-scatter.5.cloned.1.call-start = ((), (), s32[]{:S(2)}) async-start(), calls=%async_computation.4 | async-start | bytes 1843200 | tf_op jit(solution)/shard_map/reduce_scatter | solution.py:34
  276.3 4.1 copy-start.6
Sparse Core Ops, SparseCore 0:
  59.2 197.2 all-gather.1
  276.4 695.0 reduce-scatter.6
  975.1 38.4 reduce-scatter.4
